TPU v7x, 128 devices: a whole 4x4x4 slice. The times are simulated.
128 devices in a mesh: pipe: 2 (over core), dp: 4 (over x), tensor: 16 (over z, y).
Axes of the slice: x: 4, y: 4, z: 4, core: 2. Of those that a mesh axis runs over, the one named last changes fastest.
Arguments:
- embedded: bfloat16 [512, 4096], P('dp', 'pipe'), may hold values from -6 to 6
- rotation_scaled: float32 [4096, 4096], P(('pipe', 'dp'), 'tensor'), as said below
- value_proj: bfloat16 [2, 4096, 1024], P('pipe', 'tensor'), may hold values from -0.09375 to 0.09375
- output_proj: bfloat16 [2, 1024, 4096], P('pipe', None, 'tensor'), may hold values from -0.1875 to 0.1875
- mid_exponent: int32 [2, 1024], P('pipe'), may hold values from -3 to -1
- cotangent: bfloat16 [512, 4096], P('dp', 'tensor'), may hold values from -6 to 6
Outputs:
- rotation_next: float32 [4096, 4096], P(('pipe', 'dp'), 'tensor')
Inputs may be any that keep to these rules, and one draw needn't show every extreme that they name: rotation_scaled / sqrt(4096) is orthogonal.
All inputs are finite; a program needn't handle non-finite values.
Results may differ from a plain program's by a relative error of at most 0.017.
Values may be sent and summed in bfloat16 or wider, within the bound.
A program may use at most 64 MiB of HBM per device.

v0:
```python
import math
import jax
import jax.numpy as jnp
from jax import lax
from jax.sharding import PartitionSpec as P

D = 4096
MB = 4
TOK_MB = 32


def from_behind(shard, axis, by):
    length = lax.axis_size(axis)
    pairs = [(i, i + by) for i in range(length) if 0 <= i + by < length]
    return lax.ppermute(shard, axis, pairs)


def spread(shard, axis, root):
    mine = lax.axis_index(axis) == root
    return lax.psum(jnp.where(mine, shard, jnp.zeros_like(shard)), axis)


def local(embedded, rotation_scaled, value_proj, output_proj, mid_exponent, cotangent):
    sections = lax.axis_size("pipe")
    section_index = lax.axis_index("pipe")
    column_count = cotangent.shape[1]
    group_rows = embedded.shape[0]
    branch_units = value_proj.shape[2]
    rotation = rotation_scaled / math.sqrt(D)
    rot_rows = lax.all_gather(rotation.astype(jnp.bfloat16), "dp", axis=0, tiled=True)
    embed_part = jnp.dot(embedded, rot_rows, preferred_element_type=jnp.float32)
    start_field = lax.psum(embed_part.astype(jnp.bfloat16), "pipe").astype(jnp.float32)
    start_blocks = start_field.astype(jnp.bfloat16).reshape(MB, TOK_MB, column_count)
    target_blocks = cotangent.reshape(MB, TOK_MB, column_count)
    weight_in = value_proj[0]
    weight_out = output_proj[0]
    bounds = jnp.exp2(mid_exponent[0].astype(jnp.float32))
    lowest = -8.0 * bounds
    highest = 7.0 * bounds
    tick_total = MB + sections - 1

    def forward_tick(tick_count, loop_state):
        received, stash_h, stash_y, stash_r = loop_state
        micro_batch = tick_count - section_index
        active = (micro_batch >= 0) & (micro_batch < MB)
        position = jnp.clip(micro_batch, 0, MB - 1)
        first_input = lax.dynamic_index_in_dim(start_blocks, position, 0, keepdims=False)
        hidden = jnp.where(section_index == 0, first_input, received)
        hidden_f = hidden.astype(jnp.float32)
        partial_value = jnp.dot(hidden, weight_in, preferred_element_type=jnp.float32)
        squares = jnp.sum(hidden_f * hidden_f, axis=1)
        summed, square_total = lax.psum((partial_value, squares), "tensor")
        inv_rms = lax.rsqrt(square_total / D + 1e-05)[:, None]
        clipped = jnp.clip(inv_rms * summed, lowest, highest).astype(jnp.bfloat16)
        branch_out = jnp.dot(clipped, weight_out, preferred_element_type=jnp.float32)
        result = (hidden_f + branch_out).astype(jnp.bfloat16)
        stash_h = jnp.where(
            active, lax.dynamic_update_index_in_dim(stash_h, hidden, position, 0), stash_h
        )
        stash_y = jnp.where(
            active, lax.dynamic_update_index_in_dim(stash_y, summed, position, 0), stash_y
        )
        stash_r = jnp.where(
            active, lax.dynamic_update_index_in_dim(stash_r, inv_rms, position, 0), stash_r
        )
        received = from_behind(result, "pipe", 1)
        return (received, stash_h, stash_y, stash_r)

    forward_state = (
        jnp.zeros((TOK_MB, column_count), jnp.bfloat16),
        jnp.zeros((MB, TOK_MB, column_count), jnp.bfloat16),
        jnp.zeros((MB, TOK_MB, branch_units), jnp.float32),
        jnp.ones((MB, TOK_MB, 1), jnp.float32),
    )
    forward_state = lax.fori_loop(0, tick_total, forward_tick, forward_state)
    saved_h, saved_y, saved_r = (forward_state[1], forward_state[2], forward_state[3])

    def backward_tick(tick_count, loop_state):
        received, stash_g = loop_state
        micro_batch = tick_count - (sections - 1 - section_index)
        active = (micro_batch >= 0) & (micro_batch < MB)
        position = jnp.clip(micro_batch, 0, MB - 1)
        target = lax.dynamic_index_in_dim(target_blocks, position, 0, keepdims=False)
        incoming = jnp.where(section_index == sections - 1, target, received)
        hidden = lax.dynamic_index_in_dim(saved_h, position, 0, keepdims=False)
        summed = lax.dynamic_index_in_dim(saved_y, position, 0, keepdims=False)
        inv_rms = lax.dynamic_index_in_dim(saved_r, position, 0, keepdims=False)
        back_part = lax.dot_general(
            incoming, weight_out, (((1,), (1,)), ((), ())), preferred_element_type=jnp.float32
        )
        back_total = lax.psum(back_part, "tensor")
        gated_rows = inv_rms * summed
        inside = (gated_rows >= lowest) & (gated_rows <= highest)
        scaled_grad = (inv_rms * jnp.where(inside, back_total, 0.0)).astype(jnp.bfloat16)
        linear = lax.dot_general(
            scaled_grad, weight_in, (((1,), (1,)), ((), ())), preferred_element_type=jnp.float32
        )
        statistic = jnp.sum(scaled_grad.astype(jnp.float32) * summed, axis=1, keepdims=True)
        grad_field = (
            incoming.astype(jnp.float32)
            + linear
            - inv_rms * inv_rms / D * statistic * hidden.astype(jnp.float32)
        )
        sent_grad = grad_field.astype(jnp.bfloat16)
        stash_g = jnp.where(
            active & (section_index == 0),
            lax.dynamic_update_index_in_dim(stash_g, sent_grad, position, 0),
            stash_g,
        )
        received = from_behind(sent_grad, "pipe", -1)
        return (received, stash_g)

    backward_state = (
        jnp.zeros((TOK_MB, column_count), jnp.bfloat16),
        jnp.zeros((MB, TOK_MB, column_count), jnp.bfloat16),
    )
    backward_state = lax.fori_loop(0, tick_total, backward_tick, backward_state)
    grad_local = backward_state[1].reshape(group_rows, column_count)
    grad_all = spread(grad_local, "pipe", 0)
    value_part = lax.dot_general(
        grad_all, rot_rows, (((1,), (1,)), ((), ())), preferred_element_type=jnp.float32
    )
    embed_grad = lax.psum(value_part.astype(jnp.bfloat16), "tensor")
    back_part = jnp.dot(embed_grad, rot_rows, preferred_element_type=jnp.float32)
    turned = lax.psum(back_part.astype(jnp.bfloat16), "pipe").astype(jnp.float32)
    first_dirs = (2.0 * jnp.concatenate([turned, -start_field], axis=0)).astype(jnp.bfloat16)
    left_rows = jnp.concatenate([embedded, embed_grad], axis=0)
    right_rows = jnp.concatenate([embed_grad, -embedded], axis=0)
    partial_value = left_rows
    step_one = lax.psum_scatter(
        lax.dot_general(
            partial_value, first_dirs, (((0,), (0,)), ((), ())), preferred_element_type=jnp.float32
        ),
        "dp",
        scatter_dimension=0,
        tiled=True,
    )
    norm_total = lax.psum(jnp.sum(step_one * step_one), ("pipe", "dp", "tensor"))
    step_rate = jnp.sqrt(D / (norm_total + 1e-06))
    first_iter = rotation - 0.5 * step_rate * step_one
    iterate = (rotation + first_iter).astype(jnp.bfloat16)
    iter_rows = lax.all_gather(iterate, "dp", axis=0, tiled=True)
    second_part = jnp.dot(right_rows, iter_rows, preferred_element_type=jnp.float32)
    second_dirs = lax.psum(second_part.astype(jnp.bfloat16), "pipe")
    partial_value = left_rows
    step_two = lax.psum_scatter(
        lax.dot_general(
            partial_value, second_dirs, (((0,), (0,)), ((), ())), preferred_element_type=jnp.float32
        ),
        "dp",
        scatter_dimension=0,
        tiled=True,
    )
    return math.sqrt(D) * (rotation - 0.5 * step_rate * step_two)


def solution(mesh):
    return jax.shard_map(
        local,
        mesh=mesh,
        in_specs=(
            P("dp", "pipe"),
            P(("pipe", "dp"), "tensor"),
            P("pipe", "tensor", None),
            P("pipe", None, "tensor"),
            P("pipe", None),
            P("dp", "tensor"),
        ),
        out_specs=P(("pipe", "dp"), "tensor"),
        check_vma=False,
    )
```

profile of v0, /device:TPU:1, one launch (start us, length us, event | category | flops | bytes accessed | tf_op | source)
XLA Modules:
  0.0 1303.0 jit_solution(10443372473404619989)
XLA Ops:
  6.5 1.9 multiply_convert_fusion.1
  8.5 25.7 %all-gather.3.cloned.1.call-done = bf16[2048,256]{1,0:T(8,128)(2,1)} async-done(((bf16[512,256]{1,0:T(8,128)(2,1)}), bf16[2048,256]{1,0:T(8,128)(2,1)}) %all-gather.3.cloned.1.call-update) | async-done | bytes 1048592 | tf_op jit(solution)/shard_map/all_gather | solution.py:30
  34.2 2.5 fusion.14
  36.8 26.2 %all-reduce.8.cloned.1.call-done = bf16[128,256]{0,1:T(8,128)(2,1)} async-done(((bf16[128,256]{0,1:T(8,128)(2,1)}), bf16[128,256]{0,1:T(8,128)(2,1)}) %all-reduce.8.cloned.1.call-update) | async-done | bytes 65552 | tf_op jit(solution)/shard_map/psum | solution.py:32
  64.1 450.8 %while.37 = (s32[]{:T(128)}, bf16[32,256]{1,0:T(8,128)(2,1)S(1)}, bf16[4,32,256]{2,1,0:T(8,128)(2,1)S(1)}, f32[4,32,1024]{2,1,0:T(8,128)S(1)}, f32[4,32,1]{1,2,0...) while((s32[]{:T(128)}, bf16[32,256]{1,0:T(8,128)(2,1)S(1)}, ...), condition=%wide.region_5.6_spmd, body=%wide.region_1.5_spmd.sunk | while | flops 33882280 | bytes 2710062 | solution.py:75
  65.2 33.6 %psum.89 = f32[32]{0:T(128)S(1)} all-reduce(f32[32]{0:T(128)S(1)} %fusion.65), channel_id=1, replica_groups=mesh['pipe'=2,'dp'=4,'tensor'=16] {'tensor'}, use_global_device_ids=true, to_apply=%region_3.3 | all-reduce | flops 32 | bytes 256 | tf_op jit(solution)/shard_map/while/body/eval_jaxpr/psum | solution.py:52
  98.8 51.7 %all-reduce.18.cloned.1.call-done = f32[32,1024]{1,0:T(8,128)} async-done(((f32[32,1024]{1,0:T(8,128)}), f32[32,1024]{1,0:T(8,128)}) %all-reduce.18.cloned.1.call-update) | async-done | bytes 131088 | tf_op jit(solution)/shard_map/while/body/eval_jaxpr/psum | solution.py:52
  151.6 1.3 collective-permute-start
  153.8 2.3 collective-permute-done
  157.1 30.9 %psum.89 = f32[32]{0:T(128)S(1)} all-reduce(f32[32]{0:T(128)S(1)} %fusion.65), channel_id=1, replica_groups=mesh['pipe'=2,'dp'=4,'tensor'=16] {'tensor'}, use_global_device_ids=true, to_apply=%region_3.3 | all-reduce | flops 32 | bytes 256 | tf_op jit(solution)/shard_map/while/body/eval_jaxpr/psum | solution.py:52
  188.0 52.1 %all-reduce.18.cloned.1.call-done = f32[32,1024]{1,0:T(8,128)} async-done(((f32[32,1024]{1,0:T(8,128)}), f32[32,1024]{1,0:T(8,128)}) %all-reduce.18.cloned.1.call-update) | async-done | bytes 131088 | tf_op jit(solution)/shard_map/while/body/eval_jaxpr/psum | solution.py:52
  243.5 2.3 collective-permute-done
  246.7 30.9 %psum.89 = f32[32]{0:T(128)S(1)} all-reduce(f32[32]{0:T(128)S(1)} %fusion.65), channel_id=1, replica_groups=mesh['pipe'=2,'dp'=4,'tensor'=16] {'tensor'}, use_global_device_ids=true, to_apply=%region_3.3 | all-reduce | flops 32 | bytes 256 | tf_op jit(solution)/shard_map/while/body/eval_jaxpr/psum | solution.py:52
  277.6 52.1 %all-reduce.18.cloned.1.call-done = f32[32,1024]{1,0:T(8,128)} async-done(((f32[32,1024]{1,0:T(8,128)}), f32[32,1024]{1,0:T(8,128)}) %all-reduce.18.cloned.1.call-update) | async-done | bytes 131088 | tf_op jit(solution)/shard_map/while/body/eval_jaxpr/psum | solution.py:52
  333.1 2.3 collective-permute-done
  336.3 30.9 %psum.89 = f32[32]{0:T(128)S(1)} all-reduce(f32[32]{0:T(128)S(1)} %fusion.65), channel_id=1, replica_groups=mesh['pipe'=2,'dp'=4,'tensor'=16] {'tensor'}, use_global_device_ids=true, to_apply=%region_3.3 | all-reduce | flops 32 | bytes 256 | tf_op jit(solution)/shard_map/while/body/eval_jaxpr/psum | solution.py:52
  367.2 52.1 %all-reduce.18.cloned.1.call-done = f32[32,1024]{1,0:T(8,128)} async-done(((f32[32,1024]{1,0:T(8,128)}), f32[32,1024]{1,0:T(8,128)}) %all-reduce.18.cloned.1.call-update) | async-done | bytes 131088 | tf_op jit(solution)/shard_map/while/body/eval_jaxpr/psum | solution.py:52
  422.7 2.3 collective-permute-done
  426.0 30.9 %psum.89 = f32[32]{0:T(128)S(1)} all-reduce(f32[32]{0:T(128)S(1)} %fusion.65), channel_id=1, replica_groups=mesh['pipe'=2,'dp'=4,'tensor'=16] {'tensor'}, use_global_device_ids=true, to_apply=%region_3.3 | all-reduce | flops 32 | bytes 256 | tf_op jit(solution)/shard_map/while/body/eval_jaxpr/psum | solution.py:52
  456.9 52.4 %all-reduce.18.cloned.1.call-done = f32[32,1024]{1,0:T(8,128)} async-done(((f32[32,1024]{1,0:T(8,128)}), f32[32,1024]{1,0:T(8,128)}) %all-reduce.18.cloned.1.call-update) | async-done | bytes 131088 | tf_op jit(solution)/shard_map/while/body/eval_jaxpr/psum | solution.py:52
  512.6 2.3 collective-permute-done
  514.9 454.3 %while.38 = (s32[]{:T(128)}, bf16[32,256]{1,0:T(8,128)(2,1)S(1)}, bf16[4,32,256]{2,1,0:T(8,128)(2,1)S(1)}, pred[]{:T(512)}, s32[]{:T(128)}, /*index=5*/bf16[4,32...) while((s32[]{:T(128)}, bf16[32,256]{1,0:T(8,128)(2,1)S(1)}, ...), condition=%wide.region_9.10_spmd, body=%wide.region_6.9_spmd.sunk | while | flops 33988680 | bytes 2565832 | solution.py:117
  515.9 83.2 %all-reduce.20.cloned.1.call-done = f32[32,1024]{1,0:T(8,128)} async-done(((f32[32,1024]{1,0:T(8,128)}), f32[32,1024]{1,0:T(8,128)}) %all-reduce.20.cloned.1.call-update) | async-done | bytes 131088 | tf_op jit(solution)/shard_map/while/body/eval_jaxpr/psum | solution.py:91
  600.6 4.4 collective-permute-start.1
  606.8 83.3 %all-reduce.20.cloned.1.call-done = f32[32,1024]{1,0:T(8,128)} async-done(((f32[32,1024]{1,0:T(8,128)}), f32[32,1024]{1,0:T(8,128)}) %all-reduce.20.cloned.1.call-update) | async-done | bytes 131088 | tf_op jit(solution)/shard_map/while/body/eval_jaxpr/psum | solution.py:91
  691.6 4.4 collective-permute-start.1
  697.8 83.0 %all-reduce.20.cloned.1.call-done = f32[32,1024]{1,0:T(8,128)} async-done(((f32[32,1024]{1,0:T(8,128)}), f32[32,1024]{1,0:T(8,128)}) %all-reduce.20.cloned.1.call-update) | async-done | bytes 131088 | tf_op jit(solution)/shard_map/while/body/eval_jaxpr/psum | solution.py:91
  782.2 4.4 collective-permute-start.1
  788.5 83.3 %all-reduce.20.cloned.1.call-done = f32[32,1024]{1,0:T(8,128)} async-done(((f32[32,1024]{1,0:T(8,128)}), f32[32,1024]{1,0:T(8,128)}) %all-reduce.20.cloned.1.call-update) | async-done | bytes 131088 | tf_op jit(solution)/shard_map/while/body/eval_jaxpr/psum | solution.py:91
  873.2 4.4 collective-permute-start.1
  879.4 83.0 %all-reduce.20.cloned.1.call-done = f32[32,1024]{1,0:T(8,128)} async-done(((f32[32,1024]{1,0:T(8,128)}), f32[32,1024]{1,0:T(8,128)}) %all-reduce.20.cloned.1.call-update) | async-done | bytes 131088 | tf_op jit(solution)/shard_map/while/body/eval_jaxpr/psum | solution.py:91
  963.9 4.4 collective-permute-start.1
  969.9 25.1 %all-reduce.10.cloned.1.call-done = bf16[128,256]{1,0:T(8,128)(2,1)} async-done(((bf16[128,256]{1,0:T(8,128)(2,1)}), bf16[128,256]{1,0:T(8,128)(2,1)}) %all-reduce.10.cloned.1.call-update) | async-done | bytes 65552 | tf_op jit(solution)/shard_map/psum | solution.py:20
  995.0 2.1 convolution_convert_fusion
  997.4 85.5 %all-reduce.12.cloned.1.call-done = bf16[128,2048]{1,0:T(8,128)(2,1)} async-done(((bf16[128,2048]{1,0:T(8,128)(2,1)}), bf16[128,2048]{1,0:T(8,128)(2,1)}) %all-reduce.12.cloned.1.call-update) | async-done | bytes 524304 | tf_op jit(solution)/shard_map/psum | solution.py:123
  1082.8 2.2 convolution_convert_fusion.2
  1086.2 24.0 %all-reduce.14.cloned.1.call-done = bf16[128,256]{0,1:T(8,128)(2,1)} async-done(((bf16[128,256]{0,1:T(8,128)(2,1)}), bf16[128,256]{0,1:T(8,128)(2,1)}) %all-reduce.14.cloned.1.call-update) | async-done | bytes 65552 | tf_op jit(solution)/shard_map/psum | solution.py:125
  1111.1 1.8 fusion.20
  1113.0 30.7 %reduce-scatter.3.cloned.1.call-done = f32[512,256]{1,0:T(8,128)} async-done(((f32[2048,256]{1,0:T(8,128)}), f32[512,256]{1,0:T(8,128)}) %reduce-scatter.3.cloned.1.call-update) | async-done | bytes 524304 | tf_op jit(solution)/shard_map/reduce_scatter | solution.py:130
  1143.7 1.8 multiply_reduce_fusion
  1145.4 64.8 %psum.83 = f32[]{:T(128)} all-reduce(f32[]{:T(128)} %multiply_reduce_fusion), channel_id=1, replica_groups=mesh['pipe'=2,'dp'=4,'tensor'=16] {'pipe','dp','tensor'}, use_global_device_ids=true, to_apply=%region_15.16 | all-reduce | flops 1 | bytes 8 | tf_op jit(solution)/shard_map/psum | solution.py:138
  1211.0 1.8 fusion.18
  1212.9 19.4 %all-gather.5.cloned.1.call-done = bf16[2048,256]{1,0:T(8,128)(2,1)} async-done(((bf16[512,256]{1,0:T(8,128)(2,1)}), bf16[2048,256]{1,0:T(8,128)(2,1)}) %all-gather.5.cloned.1.call-update) | async-done | bytes 1048592 | tf_op jit(solution)/shard_map/all_gather | solution.py:142
  1232.3 2.3 convolution_convert_fusion.1
  1234.7 26.5 %all-reduce.16.cloned.1.call-done = bf16[256,256]{1,0:T(8,128)(2,1)} async-done(((bf16[256,256]{1,0:T(8,128)(2,1)}), bf16[256,256]{1,0:T(8,128)(2,1)}) %all-reduce.16.cloned.1.call-update) | async-done | bytes 131088 | tf_op jit(solution)/shard_map/psum | solution.py:144
  1261.1 2.7 fusion.28
  1263.9 30.7 %reduce-scatter.5.cloned.1.call-done = f32[512,256]{1,0:T(8,128)} async-done(((f32[2048,256]{1,0:T(8,128)}), f32[512,256]{1,0:T(8,128)}) %reduce-scatter.5.cloned.1.call-update) | async-done | bytes 524304 | tf_op jit(solution)/shard_map/reduce_scatter | solution.py:146
  1294.6 1.9 subtract_multiply_fusion
  (140 shorter events, 40.8 us)
Async XLA Ops:
  6.5 30.2 %copy-start.8 = (s32[1,1024]{1,0:T(1,128)S(1)}, s32[1,1024]{1,0:T(1,128)}, u32[]{:S(2)}) copy-start(s32[1,1024]{1,0:T(1,128)} %param.14) | copy-start | bytes 12292
  6.5 57.5 %copy-start.1 = (bf16[1,1024,256]{2,1,0:T(8,128)(2,1)S(1)}, bf16[1,1024,256]{2,1,0:T(8,128)(2,1)}, u32[]{:S(2)}) copy-start(bf16[1,1024,256]{2,1,0:T(8,128)(2,1)} %param.13) | copy-start | bytes 1572868
  6.5 57.5 %copy-start = (bf16[1,256,1024]{2,1,0:T(8,128)(2,1)S(1)}, bf16[1,256,1024]{2,1,0:T(8,128)(2,1)}, u32[]{:S(2)}) copy-start(bf16[1,256,1024]{2,1,0:T(8,128)(2,1)} %param.12) | copy-start | bytes 1572868
  6.5 27.7 %all-gather.3.cloned.1.call-start = ((), (), s32[]{:S(2)}) async-start(), calls=%async_computation.2 | async-start | bytes 1310720 | tf_op jit(solution)/shard_map/all_gather | solution.py:30
  8.4 54.6 %all-reduce.8.cloned.1.call-start = ((), (), s32[]{:S(2)}) async-start(), calls=%async_computation.3 | async-start | bytes 131072 | tf_op jit(solution)/shard_map/psum | solution.py:32
  64.1 450.8 %copy-start.6 = (bf16[128,256]{1,0:T(8,128)(2,1)S(1)}, bf16[128,256]{1,0:T(8,128)(2,1)}, u32[]{:S(2)}) copy-start(bf16[128,256]{1,0:T(8,128)(2,1)} %param.15) | copy-start | bytes 196612
  64.1 86.3 %all-reduce.18.cloned.1.call-start = ((), (), s32[]{:S(2)}) async-start(), calls=%async_computation.11 | async-start | bytes 262144 | tf_op jit(solution)/shard_map/while/body/eval_jaxpr/psum | solution.py:52
  151.6 4.5 collective-permute-start
  156.1 84.0 %all-reduce.18.cloned.1.call-start = ((), (), s32[]{:S(2)}) async-start(), calls=%async_computation.11 | async-start | bytes 262144 | tf_op jit(solution)/shard_map/while/body/eval_jaxpr/psum | solution.py:52
  241.2 4.5 collective-permute-start
  245.7 84.0 %all-reduce.18.cloned.1.call-start = ((), (), s32[]{:S(2)}) async-start(), calls=%async_computation.11 | async-start | bytes 262144 | tf_op jit(solution)/shard_map/while/body/eval_jaxpr/psum | solution.py:52
  330.8 4.5 collective-permute-start
  335.3 84.0 %all-reduce.18.cloned.1.call-start = ((), (), s32[]{:S(2)}) async-start(), calls=%async_computation.11 | async-start | bytes 262144 | tf_op jit(solution)/shard_map/while/body/eval_jaxpr/psum | solution.py:52
  420.5 4.5 collective-permute-start
  424.9 84.3 %all-reduce.18.cloned.1.call-start = ((), (), s32[]{:S(2)}) async-start(), calls=%async_computation.11 | async-start | bytes 262144 | tf_op jit(solution)/shard_map/while/body/eval_jaxpr/psum | solution.py:52
  510.4 4.5 collective-permute-start
  514.9 480.2 %copy-start.2 = (bf16[2048,256]{1,0:T(8,128)(2,1)S(1)}, bf16[2048,256]{1,0:T(8,128)(2,1)}, u32[]{:S(2)}) copy-start(bf16[2048,256]{1,0:T(8,128)(2,1)} %all-gather.3.cloned.1.call-done) | copy-start | bytes 3145732
  514.9 84.3 %all-reduce.20.cloned.1.call-start = ((), (), s32[]{:S(2)}) async-start(), calls=%async_computation.12 | async-start | bytes 262144 | tf_op jit(solution)/shard_map/while/body/eval_jaxpr/psum | solution.py:91
  600.6 5.3 collective-permute-start.1
  605.9 84.3 %all-reduce.20.cloned.1.call-start = ((), (), s32[]{:S(2)}) async-start(), calls=%async_computation.12 | async-start | bytes 262144 | tf_op jit(solution)/shard_map/while/body/eval_jaxpr/psum | solution.py:91
  691.6 5.3 collective-permute-start.1
  696.8 84.0 %all-reduce.20.cloned.1.call-start = ((), (), s32[]{:S(2)}) async-start(), calls=%async_computation.12 | async-start | bytes 262144 | tf_op jit(solution)/shard_map/while/body/eval_jaxpr/psum | solution.py:91
  782.2 5.3 collective-permute-start.1
  787.5 84.3 %all-reduce.20.cloned.1.call-start = ((), (), s32[]{:S(2)}) async-start(), calls=%async_computation.12 | async-start | bytes 262144 | tf_op jit(solution)/shard_map/while/body/eval_jaxpr/psum | solution.py:91
  873.2 5.3 collective-permute-start.1
  878.5 84.0 %all-reduce.20.cloned.1.call-start = ((), (), s32[]{:S(2)}) async-start(), calls=%async_computation.12 | async-start | bytes 262144 | tf_op jit(solution)/shard_map/while/body/eval_jaxpr/psum | solution.py:91
  963.9 5.3 collective-permute-start.1
  969.1 28.1 %copy-start.4 = (bf16[128,2048]{1,0:T(8,128)(2,1)S(1)}, bf16[128,2048]{1,0:T(8,128)(2,1)}, u32[]{:S(2)}) copy-start(bf16[128,2048]{1,0:T(8,128)(2,1)} %param.10) | copy-start | bytes 1572868
  969.1 28.2 %copy-start.7 = (bf16[128,256]{0,1:T(8,128)(2,1)S(1)}, bf16[128,256]{0,1:T(8,128)(2,1)}, u32[]{:S(2)}) copy-start(bf16[128,256]{0,1:T(8,128)(2,1)} %all-reduce.8.cloned.1.call-done) | copy-start | bytes 196612
  969.1 25.9 %all-reduce.10.cloned.1.call-start = ((), (), s32[]{:S(2)}) async-start(), calls=%async_computation.4 | async-start | bytes 131072 | tf_op jit(solution)/shard_map/psum | solution.py:20
  969.9 113.0 %all-reduce.12.cloned.1.call-start = ((), (), s32[]{:S(2)}) async-start(), calls=%async_computation.5 | async-start | bytes 1048576 | tf_op jit(solution)/shard_map/psum | solution.py:123
  997.2 113.1 %all-reduce.14.cloned.1.call-start = ((), (), s32[]{:S(2)}) async-start(), calls=%async_computation.6 | async-start | bytes 131072 | tf_op jit(solution)/shard_map/psum | solution.py:125
  1085.1 58.6 %reduce-scatter.3.cloned.1.call-start = ((), (), s32[]{:S(2)}) async-start(), calls=%async_computation.7 | async-start | bytes 2621440 | tf_op jit(solution)/shard_map/reduce_scatter | solution.py:130
  1112.9 98.1 %copy-start.3 = (f32[512,256]{1,0:T(8,128)S(1)}, f32[512,256]{1,0:T(8,128)}, u32[]{:S(2)}) copy-start(f32[512,256]{1,0:T(8,128)} %param.11) | copy-start | bytes 1572868
  1112.9 119.4 %copy-start.5 = (bf16[128,2048]{1,0:T(8,128)(2,1)S(1)}, bf16[128,2048]{1,0:T(8,128)(2,1)}, u32[]{:S(2)}) copy-start(bf16[128,2048]{1,0:T(8,128)(2,1)} %all-reduce.12.cloned.1.call-done) | copy-start | bytes 1572868
  1112.9 119.3 %all-gather.5.cloned.1.call-start = ((), (), s32[]{:S(2)}) async-start(), calls=%async_computation.8 | async-start | bytes 1310720 | tf_op jit(solution)/shard_map/all_gather | solution.py:142
  1212.9 48.3 %all-reduce.16.cloned.1.call-start = ((), (), s32[]{:S(2)}) async-start(), calls=%async_computation.9 | async-start | bytes 262144 | tf_op jit(solution)/shard_map/psum | solution.py:144
  1234.6 60.0 %reduce-scatter.5.cloned.1.call-start = ((), (), s32[]{:S(2)}) async-start(), calls=%async_computation.10 | async-start | bytes 2621440 | tf_op jit(solution)/shard_map/reduce_scatter | solution.py:146
Sparse Core Ops, SparseCore 0:
  9.0 25.1 all-gather.2
  36.8 26.1 all-reduce.7
  68.1 82.2 all-reduce.17
  159.8 80.2 all-reduce.17
  249.4 80.2 all-reduce.17
  339.0 80.2 all-reduce.17
  428.9 80.2 all-reduce.17
  518.9 80.2 all-reduce.19
  609.8 80.2 all-reduce.19
  700.5 80.2 all-reduce.19
  791.5 80.2 all-reduce.19
  882.1 80.2 all-reduce.19
  972.3 22.6 all-reduce.9
  998.1 84.6 all-reduce.11
  1085.2 25.0 all-reduce.13
  1113.1 30.5 reduce-scatter.2
  1213.0 19.2 all-gather.4
  1234.8 26.3 all-reduce.15
  1264.0 30.5 reduce-scatter.4
where the time goes:
time: 1300 us
  waiting for transfers between devices  986 us (76%)
  blocking collectives  222 us (17%)
  matrix products  29.6 us (2%)
  starting transfers between devices  29.1 us (2%)
  other arithmetic  20 us (2%)
  between operations  14.1 us (1%)
    psum x5, waiting for transfers between devices, backward_tick(): back_total = lax.psum(back_part, 'tensor')  416 us
    psum x5, waiting for transfers between devices, forward_tick(): summed, square_total = lax.psum((partial_value, squares), 'tensor')  260 us
    psum x5, blocking collectives, forward_tick(): summed, square_total = lax.psum((partial_value, squares), 'tensor')  157 us
    psum x1, waiting for transfers between devices, local(): embed_grad = lax.psum(value_part.astype(jnp.bfloat16), 'tensor')  85.5 us
    psum x1, blocking collectives, local(): lax.psum(jnp.sum(step_one * step_one), ('pipe', 'dp', 'tensor'))  64.8 us
    reduce_scatter x1, waiting for transfers between devices, local(): lax.psum_scatter(lax.dot_general(partial_value, second_dirs, (((0,), (0,)...  30.7 us
    reduce_scatter x1, waiting for transfers between devices, local(): lax.psum_scatter(lax.dot_general(partial_value, first_dirs, (((0,), (0,))...  30.7 us
    ppermute x10, starting transfers between devices, from_behind(): return lax.ppermute(shard, axis, pairs)  28.6 us
  transfers between devices with their start and end apart: 29, of which 29 were waited for; matrix products, arithmetic and copies ran while one was open for 1% of the time, Pallas kernels for 0%

commit v1 on v0

--- a/solution.py
+++ b/solution.py
@@ -88,7 +88,8 @@
         back_part = lax.dot_general(
             incoming, weight_out, (((1,), (1,)), ((), ())), preferred_element_type=jnp.float32
         )
-        back_total = lax.psum(back_part, "tensor")
+        blocks = lax.all_gather(back_part, "tensor", axis=0, tiled=False)
+        back_total = blocks.sum(axis=0)
         gated_rows = inv_rms * summed
         inside = (gated_rows >= lowest) & (gated_rows <= highest)
         scaled_grad = (inv_rms * jnp.where(inside, back_total, 0.0)).astype(jnp.bfloat16)

time: 1300 us -> 1110 us (0.85)
  waiting for transfers between devices: 986 us -> 791 us
    psum x5 -> x0, waiting for transfers between devices: 416 us -> none  [backward_tick(): back_total = lax.psum(back_part, 'tensor')]
    all_gather x0 -> x5, waiting for transfers between devices: none -> 221 us  [backward_tick(): blocks = lax.all_gather(back_part, 'tensor', axis=0, tiled=False)]
where the time goes in v1:
time: 1110 us
  waiting for transfers between devices  791 us (71%)
  blocking collectives  222 us (20%)
  matrix products  29.6 us (3%)
  starting transfers between devices  27.5 us (2%)
  other arithmetic  24.1 us (2%)
  between operations  14.1 us (1%)
    psum x5, waiting for transfers between devices, forward_tick(): summed, square_total = lax.psum((partial_value, squares), 'tensor')  260 us
    all_gather x5, waiting for transfers between devices, backward_tick(): blocks = lax.all_gather(back_part, 'tensor', axis=0, tiled=False)  221 us
    psum x5, blocking collectives, forward_tick(): summed, square_total = lax.psum((partial_value, squares), 'tensor')  157 us
    psum x1, waiting for transfers between devices, local(): embed_grad = lax.psum(value_part.astype(jnp.bfloat16), 'tensor')  85.5 us
    psum x1, blocking collectives, local(): lax.psum(jnp.sum(step_one * step_one), ('pipe', 'dp', 'tensor'))  64.8 us
    reduce_scatter x1, waiting for transfers between devices, local(): lax.psum_scatter(lax.dot_general(partial_value, second_dirs, (((0,), (0,)...  30.7 us
    reduce_scatter x1, waiting for transfers between devices, local(): lax.psum_scatter(lax.dot_general(partial_value, first_dirs, (((0,), (0,))...  30.7 us
    ppermute x10, starting transfers between devices, from_behind(): return lax.ppermute(shard, axis, pairs)  27.1 us
  transfers between devices with their start and end apart: 29, of which 29 were waited for; matrix products, arithmetic and copies ran while one was open for 1% of the time, Pallas kernels for 0%

profile of v1, /device:TPU:1, one launch (start us, length us, event | category | flops | bytes accessed | tf_op | source)
XLA Modules:
  0.0 1110.9 jit_solution(2361168285941676303)
XLA Ops:
  6.5 1.9 multiply_convert_fusion.1
  8.5 25.7 %all-gather.7.cloned.1.call-done = bf16[2048,256]{1,0:T(8,128)(2,1)} async-done(((bf16[512,256]{1,0:T(8,128)(2,1)}), bf16[2048,256]{1,0:T(8,128)(2,1)}) %all-gather.7.cloned.1.call-update) | async-done | bytes 1048592 | tf_op jit(solution)/shard_map/all_gather | solution.py:30
  34.2 2.5 fusion.14
  36.8 26.2 %all-reduce.7.cloned.1.call-done = bf16[128,256]{0,1:T(8,128)(2,1)} async-done(((bf16[128,256]{0,1:T(8,128)(2,1)}), bf16[128,256]{0,1:T(8,128)(2,1)}) %all-reduce.7.cloned.1.call-update) | async-done | bytes 65552 | tf_op jit(solution)/shard_map/psum | solution.py:32
  64.1 450.8 %while.37 = (s32[]{:T(128)}, bf16[32,256]{1,0:T(8,128)(2,1)S(1)}, bf16[4,32,256]{2,1,0:T(8,128)(2,1)S(1)}, f32[4,32,1024]{2,1,0:T(8,128)S(1)}, f32[4,32,1]{1,2,0...) while((s32[]{:T(128)}, bf16[32,256]{1,0:T(8,128)(2,1)S(1)}, ...), condition=%wide.region_5.6_spmd, body=%wide.region_1.5_spmd.sunk | while | flops 33882280 | bytes 2710062 | solution.py:75
  65.2 33.6 %psum.75 = f32[32]{0:T(128)S(1)} all-reduce(f32[32]{0:T(128)S(1)} %fusion.65), channel_id=1, replica_groups=mesh['pipe'=2,'dp'=4,'tensor'=16] {'tensor'}, use_global_device_ids=true, to_apply=%region_3.3 | all-reduce | flops 32 | bytes 256 | tf_op jit(solution)/shard_map/while/body/eval_jaxpr/psum | solution.py:52
  98.8 51.7 %all-reduce.17.cloned.1.call-done = f32[32,1024]{1,0:T(8,128)} async-done(((f32[32,1024]{1,0:T(8,128)}), f32[32,1024]{1,0:T(8,128)}) %all-reduce.17.cloned.1.call-update) | async-done | bytes 131088 | tf_op jit(solution)/shard_map/while/body/eval_jaxpr/psum | solution.py:52
  153.8 2.3 collective-permute-done
  157.1 30.9 %psum.75 = f32[32]{0:T(128)S(1)} all-reduce(f32[32]{0:T(128)S(1)} %fusion.65), channel_id=1, replica_groups=mesh['pipe'=2,'dp'=4,'tensor'=16] {'tensor'}, use_global_device_ids=true, to_apply=%region_3.3 | all-reduce | flops 32 | bytes 256 | tf_op jit(solution)/shard_map/while/body/eval_jaxpr/psum | solution.py:52
  188.0 52.1 %all-reduce.17.cloned.1.call-done = f32[32,1024]{1,0:T(8,128)} async-done(((f32[32,1024]{1,0:T(8,128)}), f32[32,1024]{1,0:T(8,128)}) %all-reduce.17.cloned.1.call-update) | async-done | bytes 131088 | tf_op jit(solution)/shard_map/while/body/eval_jaxpr/psum | solution.py:52
  243.5 2.3 collective-permute-done
  246.7 30.9 %psum.75 = f32[32]{0:T(128)S(1)} all-reduce(f32[32]{0:T(128)S(1)} %fusion.65), channel_id=1, replica_groups=mesh['pipe'=2,'dp'=4,'tensor'=16] {'tensor'}, use_global_device_ids=true, to_apply=%region_3.3 | all-reduce | flops 32 | bytes 256 | tf_op jit(solution)/shard_map/while/body/eval_jaxpr/psum | solution.py:52
  277.6 52.1 %all-reduce.17.cloned.1.call-done = f32[32,1024]{1,0:T(8,128)} async-done(((f32[32,1024]{1,0:T(8,128)}), f32[32,1024]{1,0:T(8,128)}) %all-reduce.17.cloned.1.call-update) | async-done | bytes 131088 | tf_op jit(solution)/shard_map/while/body/eval_jaxpr/psum | solution.py:52
  333.1 2.3 collective-permute-done
  336.3 30.9 %psum.75 = f32[32]{0:T(128)S(1)} all-reduce(f32[32]{0:T(128)S(1)} %fusion.65), channel_id=1, replica_groups=mesh['pipe'=2,'dp'=4,'tensor'=16] {'tensor'}, use_global_device_ids=true, to_apply=%region_3.3 | all-reduce | flops 32 | bytes 256 | tf_op jit(solution)/shard_map/while/body/eval_jaxpr/psum | solution.py:52
  367.2 52.1 %all-reduce.17.cloned.1.call-done = f32[32,1024]{1,0:T(8,128)} async-done(((f32[32,1024]{1,0:T(8,128)}), f32[32,1024]{1,0:T(8,128)}) %all-reduce.17.cloned.1.call-update) | async-done | bytes 131088 | tf_op jit(solution)/shard_map/while/body/eval_jaxpr/psum | solution.py:52
  422.7 2.3 collective-permute-done
  426.0 30.9 %psum.75 = f32[32]{0:T(128)S(1)} all-reduce(f32[32]{0:T(128)S(1)} %fusion.65), channel_id=1, replica_groups=mesh['pipe'=2,'dp'=4,'tensor'=16] {'tensor'}, use_global_device_ids=true, to_apply=%region_3.3 | all-reduce | flops 32 | bytes 256 | tf_op jit(solution)/shard_map/while/body/eval_jaxpr/psum | solution.py:52
  456.9 52.4 %all-reduce.17.cloned.1.call-done = f32[32,1024]{1,0:T(8,128)} async-done(((f32[32,1024]{1,0:T(8,128)}), f32[32,1024]{1,0:T(8,128)}) %all-reduce.17.cloned.1.call-update) | async-done | bytes 131088 | tf_op jit(solution)/shard_map/while/body/eval_jaxpr/psum | solution.py:52
  512.6 2.3 collective-permute-done
  514.9 262.2 %while.38 = (s32[]{:T(128)}, bf16[32,256]{1,0:T(8,128)(2,1)S(1)}, bf16[4,32,256]{2,1,0:T(8,128)(2,1)S(1)}, pred[]{:T(512)}, s32[]{:T(128)}, /*index=5*/bf16[4,32...) while((s32[]{:T(128)}, bf16[32,256]{1,0:T(8,128)(2,1)S(1)}, ...), condition=%wide.region_9.10_spmd, body=%wide.region_6.9_spmd.sunk | while | flops 34447432 | bytes 10692308 | solution.py:118
  515.9 44.4 %all-gather.11.cloned.1.call-done = f32[512,1024]{1,0:T(8,128)} async-done(((f32[32,1024]{1,0:T(8,128)}), f32[512,1024]{1,0:T(8,128)}) %all-gather.11.cloned.1.call-update) | async-done | bytes 2097168 | tf_op jit(solution)/shard_map/while/body/eval_jaxpr/all_gather | solution.py:91
  560.3 1.7 reduce_sum.62
  562.5 4.1 collective-permute-start.1
  568.4 44.4 %all-gather.11.cloned.1.call-done = f32[512,1024]{1,0:T(8,128)} async-done(((f32[32,1024]{1,0:T(8,128)}), f32[512,1024]{1,0:T(8,128)}) %all-gather.11.cloned.1.call-update) | async-done | bytes 2097168 | tf_op jit(solution)/shard_map/while/body/eval_jaxpr/all_gather | solution.py:91
  615.1 4.1 collective-permute-start.1
  621.0 44.1 %all-gather.11.cloned.1.call-done = f32[512,1024]{1,0:T(8,128)} async-done(((f32[32,1024]{1,0:T(8,128)}), f32[512,1024]{1,0:T(8,128)}) %all-gather.11.cloned.1.call-update) | async-done | bytes 2097168 | tf_op jit(solution)/shard_map/while/body/eval_jaxpr/all_gather | solution.py:91
  667.3 4.1 collective-permute-start.1
  673.3 44.4 %all-gather.11.cloned.1.call-done = f32[512,1024]{1,0:T(8,128)} async-done(((f32[32,1024]{1,0:T(8,128)}), f32[512,1024]{1,0:T(8,128)}) %all-gather.11.cloned.1.call-update) | async-done | bytes 2097168 | tf_op jit(solution)/shard_map/while/body/eval_jaxpr/all_gather | solution.py:91
  719.9 4.1 collective-permute-start.1
  725.8 44.1 %all-gather.11.cloned.1.call-done = f32[512,1024]{1,0:T(8,128)} async-done(((f32[32,1024]{1,0:T(8,128)}), f32[512,1024]{1,0:T(8,128)}) %all-gather.11.cloned.1.call-update) | async-done | bytes 2097168 | tf_op jit(solution)/shard_map/while/body/eval_jaxpr/all_gather | solution.py:91
  772.1 4.1 collective-permute-start.1
  777.9 25.1 %all-reduce.9.cloned.1.call-done = bf16[128,256]{1,0:T(8,128)(2,1)} async-done(((bf16[128,256]{1,0:T(8,128)(2,1)}), bf16[128,256]{1,0:T(8,128)(2,1)}) %all-reduce.9.cloned.1.call-update) | async-done | bytes 65552 | tf_op jit(solution)/shard_map/psum | solution.py:20
  802.9 2.1 convolution_convert_fusion
  805.3 85.5 %all-reduce.11.cloned.1.call-done = bf16[128,2048]{1,0:T(8,128)(2,1)} async-done(((bf16[128,2048]{1,0:T(8,128)(2,1)}), bf16[128,2048]{1,0:T(8,128)(2,1)}) %all-reduce.11.cloned.1.call-update) | async-done | bytes 524304 | tf_op jit(solution)/shard_map/psum | solution.py:124
  890.7 2.2 convolution_convert_fusion.2
  894.1 24.0 %all-reduce.13.cloned.1.call-done = bf16[128,256]{0,1:T(8,128)(2,1)} async-done(((bf16[128,256]{0,1:T(8,128)(2,1)}), bf16[128,256]{0,1:T(8,128)(2,1)}) %all-reduce.13.cloned.1.call-update) | async-done | bytes 65552 | tf_op jit(solution)/shard_map/psum | solution.py:126
  919.0 1.8 fusion.20
  920.9 30.7 %reduce-scatter.3.cloned.1.call-done = f32[512,256]{1,0:T(8,128)} async-done(((f32[2048,256]{1,0:T(8,128)}), f32[512,256]{1,0:T(8,128)}) %reduce-scatter.3.cloned.1.call-update) | async-done | bytes 524304 | tf_op jit(solution)/shard_map/reduce_scatter | solution.py:131
  951.6 1.8 multiply_reduce_fusion
  953.3 64.8 %psum.70 = f32[]{:T(128)} all-reduce(f32[]{:T(128)} %multiply_reduce_fusion), channel_id=1, replica_groups=mesh['pipe'=2,'dp'=4,'tensor'=16] {'pipe','dp','tensor'}, use_global_device_ids=true, to_apply=%region_15.16 | all-reduce | flops 1 | bytes 8 | tf_op jit(solution)/shard_map/psum | solution.py:139
  1018.9 1.8 fusion.18
  1020.8 19.4 %all-gather.9.cloned.1.call-done = bf16[2048,256]{1,0:T(8,128)(2,1)} async-done(((bf16[512,256]{1,0:T(8,128)(2,1)}), bf16[2048,256]{1,0:T(8,128)(2,1)}) %all-gather.9.cloned.1.call-update) | async-done | bytes 1048592 | tf_op jit(solution)/shard_map/all_gather | solution.py:143
  1040.2 2.3 convolution_convert_fusion.1
  1042.6 26.5 %all-reduce.15.cloned.1.call-done = bf16[256,256]{1,0:T(8,128)(2,1)} async-done(((bf16[256,256]{1,0:T(8,128)(2,1)}), bf16[256,256]{1,0:T(8,128)(2,1)}) %all-reduce.15.cloned.1.call-update) | async-done | bytes 131088 | tf_op jit(solution)/shard_map/psum | solution.py:145
  1069.0 2.7 fusion.28
  1071.8 30.7 %reduce-scatter.5.cloned.1.call-done = f32[512,256]{1,0:T(8,128)} async-done(((f32[2048,256]{1,0:T(8,128)}), f32[512,256]{1,0:T(8,128)}) %reduce-scatter.5.cloned.1.call-update) | async-done | bytes 524304 | tf_op jit(solution)/shard_map/reduce_scatter | solution.py:147
  1102.5 1.9 subtract_multiply_fusion
  (145 shorter events, 44.5 us)
Async XLA Ops:
  6.5 30.2 %copy-start.8 = (s32[1,1024]{1,0:T(1,128)S(1)}, s32[1,1024]{1,0:T(1,128)}, u32[]{:S(2)}) copy-start(s32[1,1024]{1,0:T(1,128)} %param.14) | copy-start | bytes 12292
  6.5 57.5 %copy-start.1 = (bf16[1,1024,256]{2,1,0:T(8,128)(2,1)S(1)}, bf16[1,1024,256]{2,1,0:T(8,128)(2,1)}, u32[]{:S(2)}) copy-start(bf16[1,1024,256]{2,1,0:T(8,128)(2,1)} %param.13) | copy-start | bytes 1572868
  6.5 57.5 %copy-start = (bf16[1,256,1024]{2,1,0:T(8,128)(2,1)S(1)}, bf16[1,256,1024]{2,1,0:T(8,128)(2,1)}, u32[]{:S(2)}) copy-start(bf16[1,256,1024]{2,1,0:T(8,128)(2,1)} %param.12) | copy-start | bytes 1572868
  6.5 27.7 %all-gather.7.cloned.1.call-start = ((), (), s32[]{:S(2)}) async-start(), calls=%async_computation.2 | async-start | bytes 1310720 | tf_op jit(solution)/shard_map/all_gather | solution.py:30
  8.4 54.6 %all-reduce.7.cloned.1.call-start = ((), (), s32[]{:S(2)}) async-start(), calls=%async_computation.3 | async-start | bytes 131072 | tf_op jit(solution)/shard_map/psum | solution.py:32
  64.1 450.8 %copy-start.6 = (bf16[128,256]{1,0:T(8,128)(2,1)S(1)}, bf16[128,256]{1,0:T(8,128)(2,1)}, u32[]{:S(2)}) copy-start(bf16[128,256]{1,0:T(8,128)(2,1)} %param.15) | copy-start | bytes 196612
  64.1 86.3 %all-reduce.17.cloned.1.call-start = ((), (), s32[]{:S(2)}) async-start(), calls=%async_computation.11 | async-start | bytes 262144 | tf_op jit(solution)/shard_map/while/body/eval_jaxpr/psum | solution.py:52
  151.6 4.5 collective-permute-start
  156.1 84.0 %all-reduce.17.cloned.1.call-start = ((), (), s32[]{:S(2)}) async-start(), calls=%async_computation.11 | async-start | bytes 262144 | tf_op jit(solution)/shard_map/while/body/eval_jaxpr/psum | solution.py:52
  241.2 4.5 collective-permute-start
  245.7 84.0 %all-reduce.17.cloned.1.call-start = ((), (), s32[]{:S(2)}) async-start(), calls=%async_computation.11 | async-start | bytes 262144 | tf_op jit(solution)/shard_map/while/body/eval_jaxpr/psum | solution.py:52
  330.8 4.5 collective-permute-start
  335.3 84.0 %all-reduce.17.cloned.1.call-start = ((), (), s32[]{:S(2)}) async-start(), calls=%async_computation.11 | async-start | bytes 262144 | tf_op jit(solution)/shard_map/while/body/eval_jaxpr/psum | solution.py:52
  420.5 4.5 collective-permute-start
  424.9 84.3 %all-reduce.17.cloned.1.call-start = ((), (), s32[]{:S(2)}) async-start(), calls=%async_computation.11 | async-start | bytes 262144 | tf_op jit(solution)/shard_map/while/body/eval_jaxpr/psum | solution.py:52
  510.4 4.5 collective-permute-start
  514.9 288.1 %copy-start.2 = (bf16[2048,256]{1,0:T(8,128)(2,1)S(1)}, bf16[2048,256]{1,0:T(8,128)(2,1)}, u32[]{:S(2)}) copy-start(bf16[2048,256]{1,0:T(8,128)(2,1)} %all-gather.7.cloned.1.call-done) | copy-start | bytes 3145732
  514.9 45.4 %all-gather.11.cloned.1.call-start = ((), (), s32[]{:S(2)}) async-start(), calls=%async_computation.12 | async-start | bytes 2228224 | tf_op jit(solution)/shard_map/while/body/eval_jaxpr/all_gather | solution.py:91
  562.5 5.0 collective-permute-start.1
  567.5 45.4 %all-gather.11.cloned.1.call-start = ((), (), s32[]{:S(2)}) async-start(), calls=%async_computation.12 | async-start | bytes 2228224 | tf_op jit(solution)/shard_map/while/body/eval_jaxpr/all_gather | solution.py:91
  615.1 5.0 collective-permute-start.1
  620.0 45.1 %all-gather.11.cloned.1.call-start = ((), (), s32[]{:S(2)}) async-start(), calls=%async_computation.12 | async-start | bytes 2228224 | tf_op jit(solution)/shard_map/while/body/eval_jaxpr/all_gather | solution.py:91
  667.3 5.0 collective-permute-start.1
  672.3 45.4 %all-gather.11.cloned.1.call-start = ((), (), s32[]{:S(2)}) async-start(), calls=%async_computation.12 | async-start | bytes 2228224 | tf_op jit(solution)/shard_map/while/body/eval_jaxpr/all_gather | solution.py:91
  719.9 5.0 collective-permute-start.1
  724.8 45.1 %all-gather.11.cloned.1.call-start = ((), (), s32[]{:S(2)}) async-start(), calls=%async_computation.12 | async-start | bytes 2228224 | tf_op jit(solution)/shard_map/while/body/eval_jaxpr/all_gather | solution.py:91
  772.1 4.9 collective-permute-start.1
  777.1 28.0 %copy-start.4 = (bf16[128,2048]{1,0:T(8,128)(2,1)S(1)}, bf16[128,2048]{1,0:T(8,128)(2,1)}, u32[]{:S(2)}) copy-start(bf16[128,2048]{1,0:T(8,128)(2,1)} %param.10) | copy-start | bytes 1572868
  777.1 28.2 %copy-start.7 = (bf16[128,256]{0,1:T(8,128)(2,1)S(1)}, bf16[128,256]{0,1:T(8,128)(2,1)}, u32[]{:S(2)}) copy-start(bf16[128,256]{0,1:T(8,128)(2,1)} %all-reduce.7.cloned.1.call-done) | copy-start | bytes 196612
  777.1 25.8 %all-reduce.9.cloned.1.call-start = ((), (), s32[]{:S(2)}) async-start(), calls=%async_computation.4 | async-start | bytes 131072 | tf_op jit(solution)/shard_map/psum | solution.py:20
  777.8 112.9 %all-reduce.11.cloned.1.call-start = ((), (), s32[]{:S(2)}) async-start(), calls=%async_computation.5 | async-start | bytes 1048576 | tf_op jit(solution)/shard_map/psum | solution.py:124
  805.1 113.1 %all-reduce.13.cloned.1.call-start = ((), (), s32[]{:S(2)}) async-start(), calls=%async_computation.6 | async-start | bytes 131072 | tf_op jit(solution)/shard_map/psum | solution.py:126
  893.0 58.6 %reduce-scatter.3.cloned.1.call-start = ((), (), s32[]{:S(2)}) async-start(), calls=%async_computation.7 | async-start | bytes 2621440 | tf_op jit(solution)/shard_map/reduce_scatter | solution.py:131
  920.8 98.1 %copy-start.3 = (f32[512,256]{1,0:T(8,128)S(1)}, f32[512,256]{1,0:T(8,128)}, u32[]{:S(2)}) copy-start(f32[512,256]{1,0:T(8,128)} %param.11) | copy-start | bytes 1572868
  920.8 119.4 %copy-start.5 = (bf16[128,2048]{1,0:T(8,128)(2,1)S(1)}, bf16[128,2048]{1,0:T(8,128)(2,1)}, u32[]{:S(2)}) copy-start(bf16[128,2048]{1,0:T(8,128)(2,1)} %all-reduce.11.cloned.1.call-done) | copy-start | bytes 1572868
  920.8 119.3 %all-gather.9.cloned.1.call-start = ((), (), s32[]{:S(2)}) async-start(), calls=%async_computation.8 | async-start | bytes 1310720 | tf_op jit(solution)/shard_map/all_gather | solution.py:143
  1020.8 48.3 %all-reduce.15.cloned.1.call-start = ((), (), s32[]{:S(2)}) async-start(), calls=%async_computation.9 | async-start | bytes 262144 | tf_op jit(solution)/shard_map/psum | solution.py:145
  1042.5 60.0 %reduce-scatter.5.cloned.1.call-start = ((), (), s32[]{:S(2)}) async-start(), calls=%async_computation.10 | async-start | bytes 2621440 | tf_op jit(solution)/shard_map/reduce_scatter | solution.py:147
Sparse Core Ops, SparseCore 0:
  9.0 25.1 all-gather.6
  36.8 26.1 all-reduce.6
  68.1 82.2 all-reduce.16
  159.8 80.2 all-reduce.16
  249.4 80.2 all-reduce.16
  339.0 80.2 all-reduce.16
  428.9 80.2 all-reduce.16
  517.9 42.3 all-gather.10
  570.4 42.3 all-gather.10
  622.7 42.3 all-gather.10
  675.2 42.3 all-gather.10
  727.5 42.3 all-gather.10
  780.3 22.6 all-reduce.8
  806.0 84.6 all-reduce.10
  893.1 25.0 all-reduce.12
  921.0 30.5 reduce-scatter.2
  1020.9 19.2 all-gather.8
  1042.6 26.3 all-reduce.14
  1071.9 30.5 reduce-scatter.4
